TPU v7x, 32 devices: a whole 2x2x4 slice. The times are simulated.
32 devices in a mesh: dp: 16 (over z, y, x), tensor: 2 (over core).
Axes of the slice: x: 2, y: 2, z: 4, core: 2. Of those that a mesh axis runs over, the one named last changes fastest.
Arguments:
- tokens: bfloat16 [2, 16, 256, 768], P(None, 'dp', 'tensor'), may hold values from -6 to 6
- lengths: int32 [2, 16, 8], P(None, 'dp'), may hold values from 1 to 64, 256 in all within a row
- qkv_weight: bfloat16 [2, 3, 768, 768], P(None, None, 'dp', 'tensor'), may hold values from -0.21875 to 0.21875
- qkv_bias: bfloat16 [2, 2, 2, 384], P(None, None, 'tensor', 'dp'), may hold values from -3 to 3
- out_weight: bfloat16 [2, 768, 768], P(None, 'tensor', 'dp'), may hold values from -0.875 to 0.875
- up_weight: bfloat16 [2, 768, 3072], P(None, 'dp', 'tensor'), may hold values from -0.21875 to 0.21875
- up_bias: bfloat16 [2, 2, 1536], P(None, 'tensor', 'dp'), may hold values from -3 to 3
- down_weight: bfloat16 [2, 3072, 768], P(None, 'tensor', 'dp'), may hold values from -0.109375 to 0.109375
- norm_gains: bfloat16 [2, 2, 768], P(None, None, 'dp'), may hold values from 0.5 to 1.5
- shifts: bfloat16 [2, 4, 768], P(None, None, 'dp'), may hold values from -2 to 2
- cotangent: bfloat16 [2, 16, 256, 768], P(None, 'dp', 'tensor'), may hold values from -6 to 6
Outputs:
- out_tokens: float32 [2, 16, 256, 768], P(None, 'dp', 'tensor')
- token_grad: float32 [2, 16, 256, 768], P(None, 'dp', 'tensor')
- qkv_weight_grad: float32 [2, 3, 768, 768], P(None, None, 'dp', 'tensor')
- qkv_bias_grad: float32 [2, 2, 2, 384], P(None, None, 'tensor', 'dp')
- out_weight_grad: float32 [2, 768, 768], P(None, 'tensor', 'dp')
- up_weight_grad: float32 [2, 768, 3072], P(None, 'dp', 'tensor')
- up_bias_grad: float32 [2, 2, 1536], P(None, 'tensor', 'dp')
- down_weight_grad: float32 [2, 3072, 768], P(None, 'tensor', 'dp')
- gain_grad: float32 [2, 2, 768], P(None, None, 'dp')
- shift_grad: float32 [2, 4, 768], P(None, None, 'dp')
Inputs may be any that keep to these rules, and one draw needn't show every extreme that they name: The 8 lengths of a row sum to 256; in every row the longest is exactly 64.
All inputs are finite; a program needn't handle non-finite values.
Results may differ from a plain program's by a relative error of at most 0.025.
Values may be sent and summed in bfloat16 or wider, within the bound.
No kernel may reach another device: no remote copies, remote signals or barrier semaphores. Data moves between devices by JAX's collectives and lax.ppermute only.
A program may use at most 192 MiB of HBM per device.

v0:
```python
import jax
import jax.numpy as jnp
from jax import lax
from jax.sharding import PartitionSpec as P

HD = 64
LEN = 256
SQRT_HALF = 0.7071067811865476
DENSITY_SCALE = 0.3989422804014327


def fetch_each(layer_weights):
    return (
        lax.all_gather(layer_weights[0], "dp", axis=1, tiled=True),
        lax.all_gather(layer_weights[1], "dp", axis=2, tiled=True),
        lax.all_gather(layer_weights[2], "dp", axis=1, tiled=True),
        lax.all_gather(layer_weights[3], "dp", axis=0, tiled=True),
        lax.all_gather(layer_weights[4], "dp", axis=1, tiled=True),
        lax.all_gather(layer_weights[5], "dp", axis=1, tiled=True),
        lax.all_gather(layer_weights[6], "dp", axis=1, tiled=True),
        lax.all_gather(layer_weights[7], "dp", axis=1, tiled=True),
    )


def gather_rows(half_rows):
    return lax.all_gather(half_rows, "tensor", axis=0, tiled=True)


def sum_rows(term_fn, row_count):
    return lax.psum_scatter(
        term_fn(jnp.int32(0), row_count * lax.axis_size("tensor")).astype(jnp.bfloat16),
        "tensor",
        scatter_dimension=0,
        tiled=True,
    ).astype(jnp.float32)


def segment_ids(row_lengths):
    finish = jnp.cumsum(row_lengths, dtype=jnp.int32)
    places = jnp.arange(LEN, dtype=jnp.int32)
    return jnp.sum((places[:, None] >= finish[None, :]).astype(jnp.int32), axis=1, dtype=jnp.int32)


def gelu_value(widened):
    return 0.5 * widened * (1.0 + lax.erf(widened * SQRT_HALF))


def gelu_slope(widened):
    return (
        0.5 * (1.0 + lax.erf(widened * SQRT_HALF))
        + widened * jnp.exp(-0.5 * widened * widened) * DENSITY_SCALE
    )


def norm_forward(summed, gain, shift):
    center = summed - jnp.mean(summed, axis=-1, keepdims=True)
    spread = jnp.mean(center * center, axis=-1, keepdims=True)
    scaling = lax.rsqrt(spread + 1e-12)
    normal = center * scaling
    return (normal * gain.astype(jnp.float32) + shift, normal, scaling)


def norm_backward(upstream, normal, scaling, gain):
    gain_part = jnp.sum(upstream * normal, axis=0)
    shift_part = jnp.sum(upstream, axis=0)
    scaled = upstream * gain.astype(jnp.float32)
    centered = scaled - jnp.mean(scaled, axis=-1, keepdims=True)
    back = scaling * (centered - normal * jnp.mean(scaled * normal, axis=-1, keepdims=True))
    return (back, gain_part, shift_part)


def split_heads(projected):
    length = projected.shape[0]
    heads = projected.shape[2] // HD
    block = min(length, 512)
    blocks = length // block
    keys_all = projected[:, 1].reshape(length, heads, HD)
    values_all = projected[:, 2].reshape(length, heads, HD)
    queries = projected[:, 0].reshape(blocks, block, heads, HD)
    return (length, heads, block, blocks, queries, keys_all, values_all)


def attention(projected, segment):
    length, heads, block, blocks, queries, keys_all, values_all = split_heads(projected)

    def one_block(packed):
        query_block, segment_block = packed
        raw_scores = (
            jnp.einsum("qhd,khd->hqk", query_block, keys_all, preferred_element_type=jnp.float32)
            * 0.125
        )
        allowed = segment_block[:, None] == segment[None, :]
        scores = jnp.where(allowed[None], raw_scores, -1000000000.0)
        highest = jnp.max(scores, axis=-1, keepdims=True)
        raised = jnp.exp(scores - highest)
        row_total = jnp.sum(raised, axis=-1, keepdims=True)
        weights = (raised / row_total).astype(jnp.bfloat16)
        context = jnp.einsum(
            "hqk,khd->qhd", weights, values_all, preferred_element_type=jnp.float32
        )
        return (
            context.reshape(block, heads * HD).astype(jnp.bfloat16),
            (highest + jnp.log(row_total))[:, :, 0],
        )

    context, log_totals = lax.map(one_block, (queries, segment.reshape(blocks, block)))
    return (context.reshape(length, heads * HD), log_totals)


def attention_back(projected, segment, log_totals, context_grad):
    length, heads, block, blocks, queries, keys_all, values_all = split_heads(projected)
    grad_blocks = context_grad.reshape(blocks, block, heads, HD)

    def one_block(carry, packed):
        key_grad, value_grad = carry
        query_block, segment_block, log_block, grad_block = packed
        raw_scores = (
            jnp.einsum("qhd,khd->hqk", query_block, keys_all, preferred_element_type=jnp.float32)
            * 0.125
        )
        allowed = segment_block[:, None] == segment[None, :]
        scores = jnp.where(allowed[None], raw_scores, -1000000000.0)
        weights = jnp.exp(scores - log_block[:, :, None])
        value_grad = value_grad + jnp.einsum(
            "hqk,qhd->khd",
            weights.astype(jnp.bfloat16),
            grad_block,
            preferred_element_type=jnp.float32,
        )
        weight_grad = jnp.einsum(
            "qhd,khd->hqk", grad_block, values_all, preferred_element_type=jnp.float32
        )
        inner = jnp.sum(weights * weight_grad, axis=-1, keepdims=True)
        score_grad = (weights * (weight_grad - inner)).astype(jnp.bfloat16)
        query_grad = (
            jnp.einsum("hqk,khd->qhd", score_grad, keys_all, preferred_element_type=jnp.float32)
            * 0.125
        )
        key_grad = (
            key_grad
            + jnp.einsum(
                "hqk,qhd->khd", score_grad, query_block, preferred_element_type=jnp.float32
            )
            * 0.125
        )
        return ((key_grad, value_grad), query_grad.reshape(block, heads * HD).astype(jnp.bfloat16))

    start_zero = jnp.zeros((length, heads, HD), jnp.float32)
    (key_grad, value_grad), query_grad = lax.scan(
        one_block,
        (start_zero, start_zero),
        (queries, segment.reshape(blocks, block), log_totals, grad_blocks),
    )
    return jnp.stack(
        [
            query_grad.reshape(length, heads * HD),
            key_grad.reshape(length, heads * HD).astype(jnp.bfloat16),
            value_grad.reshape(length, heads * HD).astype(jnp.bfloat16),
        ],
        axis=1,
    )


def forward_layer(x_half, segment, layer_weights):
    (
        layer_qkv,
        layer_qkv_bias,
        layer_out,
        layer_up,
        layer_up_bias,
        layer_down,
        layer_gains,
        layer_shifts,
    ) = layer_weights
    half_rows = x_half.shape[0]
    entering = gather_rows(x_half.astype(jnp.bfloat16))
    projected = jnp.einsum("td,kdc->tkc", entering, layer_qkv, preferred_element_type=jnp.float32)
    bias_rows = layer_qkv_bias.reshape(2, -1).astype(jnp.float32)
    bias_all = jnp.stack([bias_rows[0], jnp.zeros_like(bias_rows[0]), bias_rows[1]])
    projected = (projected + bias_all).astype(jnp.bfloat16)
    context, log_totals = attention(projected, segment)

    def out_term(first_row, row_count):
        return jnp.dot(context, layer_out, preferred_element_type=jnp.float32)

    shift_rows = layer_shifts.astype(jnp.float32)
    first_sum = x_half + sum_rows(out_term, half_rows) + shift_rows[0]
    normed, normal_one, scale_one = norm_forward(first_sum, layer_gains[0], shift_rows[1])
    widened_in = gather_rows(normed.astype(jnp.bfloat16))
    widened = jnp.dot(
        widened_in, layer_up, preferred_element_type=jnp.float32
    ) + layer_up_bias.reshape(-1).astype(jnp.float32)
    activated = gelu_value(widened).astype(jnp.bfloat16)

    def down_term(first_row, row_count):
        return jnp.dot(activated, layer_down, preferred_element_type=jnp.float32)

    second_sum = normed + sum_rows(down_term, half_rows) + shift_rows[2]
    result, normal_two, scale_two = norm_forward(second_sum, layer_gains[1], shift_rows[3])
    stored = (
        entering,
        projected,
        context,
        log_totals,
        normal_one,
        scale_one,
        widened_in,
        widened,
        activated,
        normal_two,
        scale_two,
    )
    return (result, stored)


def backward_layer(upstream, segment, layer_weights, stored):
    (
        layer_qkv,
        layer_qkv_bias,
        layer_out,
        layer_up,
        layer_up_bias,
        layer_down,
        layer_gains,
        layer_shifts,
    ) = layer_weights
    (
        entering,
        projected,
        context,
        log_totals,
        normal_one,
        scale_one,
        widened_in,
        widened,
        activated,
        normal_two,
        scale_two,
    ) = stored
    half_rows = upstream.shape[0]
    second_grad, gain_two, shift_two = norm_backward(
        upstream, normal_two, scale_two, layer_gains[1]
    )
    down_seed = gather_rows(second_grad.astype(jnp.bfloat16))
    down_grad = jnp.einsum("tf,td->fd", activated, down_seed, preferred_element_type=jnp.float32)
    active_grad = jnp.einsum("td,fd->tf", down_seed, layer_down, preferred_element_type=jnp.float32)
    widened_grad = (active_grad * gelu_slope(widened)).astype(jnp.bfloat16)
    up_grad = jnp.einsum("td,tf->df", widened_in, widened_grad, preferred_element_type=jnp.float32)
    up_bias_grad = jnp.sum(widened_grad, axis=0, dtype=jnp.float32).reshape(1, -1)

    def up_term(first_row, row_count):
        return jnp.einsum("tf,df->td", widened_grad, layer_up, preferred_element_type=jnp.float32)

    normed_grad = second_grad + sum_rows(up_term, half_rows)
    first_grad, gain_one, shift_one = norm_backward(
        normed_grad, normal_one, scale_one, layer_gains[0]
    )
    out_seed = gather_rows(first_grad.astype(jnp.bfloat16))
    out_grad = jnp.einsum("tc,td->cd", context, out_seed, preferred_element_type=jnp.float32)
    context_grad = jnp.einsum(
        "td,cd->tc", out_seed, layer_out, preferred_element_type=jnp.float32
    ).astype(jnp.bfloat16)
    projected_grad = attention_back(projected, segment, log_totals, context_grad)
    column_sums = jnp.sum(projected_grad, axis=0, dtype=jnp.float32)
    qkv_bias_grad = jnp.stack([column_sums[0], column_sums[2]]).reshape(2, 1, -1)
    qkv_grad = jnp.einsum(
        "td,tkc->kdc", entering, projected_grad, preferred_element_type=jnp.float32
    )

    def in_term(first_row, row_count):
        return jnp.einsum(
            "tkc,kdc->td", projected_grad, layer_qkv, preferred_element_type=jnp.float32
        )

    input_grad = first_grad + sum_rows(in_term, half_rows)
    gain_grads = jnp.stack([gain_one, gain_two])
    shift_grads = jnp.stack(
        [jnp.sum(first_grad, axis=0), shift_one, jnp.sum(second_grad, axis=0), shift_two]
    )
    return (
        input_grad,
        (
            qkv_grad,
            qkv_bias_grad,
            out_grad,
            up_grad,
            up_bias_grad,
            down_grad,
            gain_grads,
            shift_grads,
        ),
    )


def on_device(
    tokens,
    lengths,
    qkv_weight,
    qkv_bias,
    out_weight,
    up_weight,
    up_bias,
    down_weight,
    norm_gains,
    shifts,
    cotangent,
):
    params = (qkv_weight, qkv_bias, out_weight, up_weight, up_bias, down_weight, norm_gains, shifts)
    layers = qkv_weight.shape[0]
    micro = tokens.shape[0]

    def layer_params(layer_index):
        return fetch_each(tuple((member[layer_index] for member in params)))

    totals = [None] * layers
    out_list = []
    grad_list = []
    for micro_index in range(micro):
        segment = segment_ids(lengths[micro_index, 0])
        hidden = tokens[micro_index, 0].astype(jnp.float32)
        stored_list = []
        for layer_index in range(layers):
            hidden, stored = forward_layer(hidden, segment, layer_params(layer_index))
            stored_list.append(stored)
        out_list.append(hidden)
        upstream = cotangent[micro_index, 0].astype(jnp.float32)
        for layer_index in reversed(range(layers)):
            upstream, layer_grads = backward_layer(
                upstream, segment, layer_params(layer_index), stored_list[layer_index]
            )
            share_part = (
                lax.psum_scatter(layer_grads[0], "dp", scatter_dimension=1, tiled=True),
                lax.psum_scatter(layer_grads[1], "dp", scatter_dimension=2, tiled=True),
                lax.psum_scatter(layer_grads[2], "dp", scatter_dimension=1, tiled=True),
                lax.psum_scatter(layer_grads[3], "dp", scatter_dimension=0, tiled=True),
                lax.psum_scatter(layer_grads[4], "dp", scatter_dimension=1, tiled=True),
                lax.psum_scatter(layer_grads[5], "dp", scatter_dimension=1, tiled=True),
                lax.psum_scatter(layer_grads[6], "dp", scatter_dimension=1, tiled=True),
                lax.psum_scatter(layer_grads[7], "dp", scatter_dimension=1, tiled=True),
            )
            totals[layer_index] = (
                share_part
                if totals[layer_index] is None
                else jax.tree.map(jnp.add, totals[layer_index], share_part)
            )
        grad_list.append(upstream)
    stacked = [
        jnp.stack([layer_total[member_index] for layer_total in totals])
        for member_index in range(8)
    ]
    gain_total, shift_total = lax.psum((stacked[6], stacked[7]), "tensor")
    return (
        jnp.stack(out_list)[:, None],
        jnp.stack(grad_list)[:, None],
        stacked[0],
        stacked[1],
        stacked[2],
        stacked[3],
        stacked[4],
        stacked[5],
        gain_total,
        shift_total,
    )


def solution(mesh):
    in_specs = (
        P(None, "dp", "tensor", None),
        P(None, "dp", None),
        P(None, None, "dp", "tensor"),
        P(None, None, "tensor", "dp"),
        P(None, "tensor", "dp"),
        P(None, "dp", "tensor"),
        P(None, "tensor", "dp"),
        P(None, "tensor", "dp"),
        P(None, None, "dp"),
        P(None, None, "dp"),
        P(None, "dp", "tensor", None),
    )
    out_specs = (
        P(None, "dp", "tensor", None),
        P(None, "dp", "tensor", None),
        P(None, None, "dp", "tensor"),
        P(None, None, "tensor", "dp"),
        P(None, "tensor", "dp"),
        P(None, "dp", "tensor"),
        P(None, "tensor", "dp"),
        P(None, "tensor", "dp"),
        P(None, None, "dp"),
        P(None, None, "dp"),
    )
    return jax.shard_map(
        on_device, mesh=mesh, in_specs=in_specs, out_specs=out_specs, check_vma=False
    )
```

profile of v0, /device:TPU:0, one launch (start us, length us, event | category | flops | bytes accessed | tf_op | source)
XLA Modules:
  0.0 2629.9 jit_solution(13975036079830027915)
XLA Ops:
  10.9 43.6 %all-gather.2 = bf16[1,2,1,384]{2,1,0,3:T(2,128)(2,1)S(1)} all-gather(bf16[1,2,1,24]{2,1,0,3:T(2,128)(2,1)S(1)} %copy.360), channel_id=4, replica_groups=mesh['dp'=16,'tensor'=2] {'dp'}, dimensions={3}, use_global_device_ids=true | all-gather | bytes 1632 | tf_op jit(solution)/shard_map/all_gather | solution.py:15
  56.3 37.4 %all-gather.10 = bf16[1,2,1,384]{2,1,0,3:T(2,128)(2,1)S(1)} all-gather(bf16[1,2,1,24]{2,1,0,3:T(2,128)(2,1)S(1)} %copy.363), channel_id=12, replica_groups=mesh['dp'=16,'tensor'=2] {'dp'}, dimensions={3}, use_global_device_ids=true | all-gather | bytes 1632 | tf_op jit(solution)/shard_map/all_gather | solution.py:15
  102.6 40.9 %all-gather.3 = bf16[1,384,768]{1,2,0:T(8,128)(2,1)S(1)} all-gather(bf16[1,384,48]{1,2,0:T(8,128)(2,1)S(1)} %get-tuple-element.417), channel_id=5, replica_groups=mesh['dp'=16,'tensor'=2] {'dp'}, dimensions={2}, use_global_device_ids=true | all-gather | bytes 626688 | tf_op jit(solution)/shard_map/all_gather | solution.py:16
  143.5 2.4 fusion.82
  166.8 38.0 %all-reduce.9 = (bf16[1536]{0:T(1024)(128)(2,1)S(1)}, bf16[1536]{0:T(1024)(128)(2,1)}) all-reduce(bf16[1536]{0:T(1024)(128)(2,1)S(1)} %dynamic-update-slice, bf16[1536]{0:T(1024)(128)(2,1)S(1)} %dynamic-update-slice.1), channel_id=9, replica_groups=mesh['dp'=16,'tensor'=2] {'dp'}, use_global_device_ids=true, to_apply=%add | all-reduce | flops 3072 | bytes 12288
  208.5 41.7 %all-gather.4 = bf16[1,4,768]{1,0,2:T(2,128)(2,1)S(1)} all-gather(bf16[1,4,48]{1,0,2:T(2,128)(2,1)} %copy.361), channel_id=6, replica_groups=mesh['dp'=16,'tensor'=2] {'dp'}, dimensions={2}, use_global_device_ids=true | all-gather | bytes 6528 | tf_op jit(solution)/shard_map/all_gather | solution.py:21
  250.5 39.1 %all-gather.5 = bf16[1,2,768]{1,0,2:T(2,128)(2,1)S(1)} all-gather(bf16[1,2,48]{1,0,2:T(2,128)(2,1)} %copy.362), channel_id=7, replica_groups=mesh['dp'=16,'tensor'=2] {'dp'}, dimensions={2}, use_global_device_ids=true | all-gather | bytes 3264 | tf_op jit(solution)/shard_map/all_gather | solution.py:20
  289.6 4.6 fusion.184
  294.3 11.0 slice_reduce_fusion.4
  313.5 3.6 convolution_add_fusion.5
  317.1 3.8 fusion.121
  323.3 4.0 multiply_convert_fusion.7
  330.5 44.5 %all-gather.11 = bf16[1,384,768]{1,2,0:T(8,128)(2,1)} all-gather(bf16[1,384,48]{1,2,0:T(8,128)(2,1)} %get-tuple-element.416), channel_id=13, replica_groups=mesh['dp'=16,'tensor'=2] {'dp'}, dimensions={2}, use_global_device_ids=true | all-gather | bytes 626688 | tf_op jit(solution)/shard_map/all_gather | solution.py:16
  382.2 19.3 all-gather.31.cloned.1.call-done
  420.9 2.6 fusion.252
  434.5 41.7 %all-gather.12 = bf16[1,4,768]{1,0,2:T(2,128)(2,1)S(1)} all-gather(bf16[1,4,48]{1,0,2:T(2,128)(2,1)} %copy.364), channel_id=14, replica_groups=mesh['dp'=16,'tensor'=2] {'dp'}, dimensions={2}, use_global_device_ids=true | all-gather | bytes 6528 | tf_op jit(solution)/shard_map/all_gather | solution.py:21
  476.6 40.0 %all-gather.13 = bf16[1,2,768]{1,0,2:T(2,128)(2,1)S(1)} all-gather(bf16[1,2,48]{1,0,2:T(2,128)(2,1)} %copy.365), channel_id=15, replica_groups=mesh['dp'=16,'tensor'=2] {'dp'}, dimensions={2}, use_global_device_ids=true | all-gather | bytes 3264 | tf_op jit(solution)/shard_map/all_gather | solution.py:20
  516.7 4.6 fusion.182
  521.3 11.5 slice_reduce_fusion
  538.4 3.7 convolution_add_fusion.4
  542.0 30.6 %all-gather.35.cloned.1.call-done = bf16[1,1536,768]{1,2,0:T(8,128)(2,1)} async-done(((bf16[1,1536,48]{1,2,0:T(8,128)(2,1)}), bf16[1,1536,768]{1,2,0:T(8,128)(2,1)}) %all-gather.35.cloned.1.call-update) | async-done | bytes 2359312 | tf_op jit(solution)/shard_map/all_gather | solution.py:19
  572.7 3.8 fusion.133
  578.8 3.9 multiply_convert_fusion.6
  586.5 7.9 reduce-scatter.49.cloned.1.call-done
  605.4 2.3 all_gather.156
  607.7 3.9 convert_reduce_fusion.1
  618.5 7.0 reduce-scatter.59.cloned.1.call-done
  625.5 3.4 fusion.219
  636.3 2.7 convolution_convert_fusion.10
  647.1 2.6 convolution_convert_fusion.6
  660.1 3.2 fusion.100
  673.3 3.3 fusion.103
  679.7 5.9 reduce-scatter.61.cloned.1.call-done
  685.7 2.6 fusion.217
  697.0 2.3 all_gather.162
  699.3 3.9 convert_reduce_fusion.2
  737.4 2.7 multiply_reduce_fusion.9
  742.8 2.5 all_gather.163
  766.6 3.0 fusion.109
  776.8 2.4 add_bitcast_fusion
  779.3 6.3 copy.318
  787.6 2.5 add_bitcast_fusion.1
  790.1 6.3 copy.315
  798.5 3.0 convolution_add_fusion.2
  803.6 3.0 convolution_add_fusion.3
  808.7 3.1 convolution_add_fusion
  813.9 3.1 convolution_add_fusion.1
  819.5 27.4 %reduce-scatter.89.cloned.1.call-done = f32[96,1]{1,0:T(8,128)} async-done(((f32[1536,1]{1,0:T(8,128)}), f32[96,1]{1,0:T(8,128)}) %reduce-scatter.89.cloned.1.call-update) | async-done | bytes 400
  848.1 125.8 %reduce-scatter.93.cloned.1.call-done = f32[48,2]{1,0:T(8,128)} async-done(((f32[768,2]{1,0:T(8,128)}), f32[48,2]{1,0:T(8,128)}) %reduce-scatter.93.cloned.1.call-update) | async-done | bytes 400
  974.7 126.9 %reduce-scatter.87.cloned.1.call-done = f32[96,1]{1,0:T(8,128)} async-done(((f32[1536,1]{1,0:T(8,128)}), f32[96,1]{1,0:T(8,128)}) %reduce-scatter.87.cloned.1.call-update) | async-done | bytes 400
  1103.1 125.4 %reduce-scatter.97.cloned.1.call-done = f32[48,4]{1,0:T(8,128)} async-done(((f32[768,4]{1,0:T(8,128)}), f32[48,4]{1,0:T(8,128)}) %reduce-scatter.97.cloned.1.call-update) | async-done | bytes 784
  1229.6 40.4 %all-reduce.6 = (f32[2,1,384]{2,0,1:T(2,128)S(1)}, f32[2,1,384]{2,0,1:T(2,128)S(1)}) all-reduce(f32[2,1,384]{2,0,1:T(2,128)S(1)} %fusion.207, f32[2,1,384]{2,0,1:T(2,128)S(1)} %fusion.206), channel_id=55, replica_groups=mesh['dp'=16,'tensor'=2] {'dp'}, use_global_device_ids=true, to_apply=%region_73.74.clone | all-reduce | flops 1536 | bytes 12288
  1270.7 84.7 %reduce-scatter.91.cloned.1.call-done = f32[48,2]{1,0:T(8,128)} async-done(((f32[768,2]{1,0:T(8,128)}), f32[48,2]{1,0:T(8,128)}) %reduce-scatter.91.cloned.1.call-update) | async-done | bytes 400
  1356.3 126.1 %reduce-scatter.95.cloned.1.call-done = f32[48,4]{1,0:T(8,128)} async-done(((f32[768,4]{1,0:T(8,128)}), f32[48,4]{1,0:T(8,128)}) %reduce-scatter.95.cloned.1.call-update) | async-done | bytes 784
  1483.2 3.1 all-reduce.8
  1486.2 5.8 reduce-scatter.73.cloned.1.call-done
  1492.9 10.2 reduce-scatter.65.cloned.1.call-done
  1505.1 129.7 %reduce-scatter.77.cloned.1.call-done = f32[384,48]{0,1:T(8,128)} async-done(((f32[384,768]{0,1:T(8,128)}), f32[384,48]{0,1:T(8,128)}) %reduce-scatter.77.cloned.1.call-update) | async-done | bytes 73744 | tf_op jit(solution)/shard_map/reduce_scatter | solution.py:334
  1634.7 129.3 %reduce-scatter.75.cloned.1.call-done = f32[384,48]{0,1:T(8,128)} async-done(((f32[384,768]{0,1:T(8,128)}), f32[384,48]{0,1:T(8,128)}) %reduce-scatter.75.cloned.1.call-update) | async-done | bytes 73744 | tf_op jit(solution)/shard_map/reduce_scatter | solution.py:334
  1765.6 282.5 %all-reduce.12.cloned.1.call-done = (f32[3,768,384]{2,0,1:T(4,128)}, f32[3,768,384]{2,0,1:T(4,128)}) async-done(((f32[3,768,384]{2,0,1:T(4,128)}, f32[3,768,384]{2,0,1:T(4,128)}), (f32[3,768,384]{2,0,1:T(4,128)}, f32[3,768,384]{2,0,1:T(4,128)})) %all-reduce.12.cloned.1.call-update) | async-done | bytes 7077904
  2051.0 140.0 %reduce-scatter.81.cloned.1.call-done = f32[48,1536]{1,0:T(8,128)} async-done(((f32[768,1536]{1,0:T(8,128)}), f32[48,1536]{1,0:T(8,128)}) %reduce-scatter.81.cloned.1.call-update) | async-done | bytes 294928 | tf_op jit(solution)/shard_map/reduce_scatter | solution.py:335
  2191.0 143.5 %reduce-scatter.79.cloned.1.call-done = f32[48,1536]{1,0:T(8,128)} async-done(((f32[768,1536]{1,0:T(8,128)}), f32[48,1536]{1,0:T(8,128)}) %reduce-scatter.79.cloned.1.call-update) | async-done | bytes 294928 | tf_op jit(solution)/shard_map/reduce_scatter | solution.py:335
  2336.3 141.6 %reduce-scatter.85.cloned.1.call-done = f32[1536,48]{0,1:T(8,128)} async-done(((f32[1536,768]{0,1:T(8,128)}), f32[1536,48]{0,1:T(8,128)}) %reduce-scatter.85.cloned.1.call-update) | async-done | bytes 294928 | tf_op jit(solution)/shard_map/reduce_scatter | solution.py:337
  2477.9 143.3 %reduce-scatter.83.cloned.1.call-done = f32[1536,48]{0,1:T(8,128)} async-done(((f32[1536,768]{0,1:T(8,128)}), f32[1536,48]{0,1:T(8,128)}) %reduce-scatter.83.cloned.1.call-update) | async-done | bytes 294928 | tf_op jit(solution)/shard_map/reduce_scatter | solution.py:337
  (753 shorter events, 260.1 us)
Async XLA Ops:
  7.2 88.3 %copy-start.4 = (bf16[2,1,128,768]{3,2,1,0:T(8,128)(2,1)S(1)}, bf16[2,1,128,768]{3,2,1,0:T(8,128)(2,1)}, u32[]{:S(2)}) copy-start(bf16[2,1,128,768]{3,2,1,0:T(8,128)(2,1)} %param.11) | copy-start | bytes 1179652
  7.2 136.3 %all-gather.25.cloned.1.call-start = ((), (), s32[]{:S(2)}) async-start(), calls=%async_computation.44 | async-start | bytes 1880064 | tf_op jit(solution)/shard_map/all_gather | solution.py:14
  9.0 296.4 %reduce-scatter.43.cloned.1.call-start = ((), (), s32[]{:S(2)}) async-start(), calls=%async_computation.28 | async-start | bytes 589824 | tf_op jit(solution)/shard_map/reduce_scatter | solution.py:30
  93.7 8.3 copy-start.140
  97.6 50.7 %copy-start.93 = (bf16[1,1,256,768]{3,2,1,0:T(8,128)(2,1)}, bf16[1,1,256,768]{3,2,1,0:T(8,128)(2,1)S(1)}, u32[]{:S(2)}) copy-start(bf16[1,1,256,768]{3,2,1,0:T(8,128)(2,1)S(1)} %all-gather) | copy-start | bytes 1179652
  99.7 46.2 %copy-start.82 = (bf16[1,1,256,768]{3,2,1,0:T(8,128)(2,1)}, bf16[1,1,256,768]{3,2,1,0:T(8,128)(2,1)S(1)}, u32[]{:S(2)}) copy-start(bf16[1,1,256,768]{3,2,1,0:T(8,128)(2,1)S(1)} %all-gather.17) | copy-start | bytes 1179652
  143.5 9.1 copy-start.5
  153.8 153.2 %reduce-scatter.51.cloned.1.call-start = ((), (), s32[]{:S(2)}) async-start(), calls=%async_computation.32 | async-start | bytes 589824 | tf_op jit(solution)/shard_map/reduce_scatter | solution.py:30
  158.4 46.9 %copy-start.184 = (bf16[2,4,48]{2,1,0:T(4,128)(2,1)S(1)}, bf16[2,4,48]{2,1,0:T(4,128)(2,1)}, u32[]{:S(2)}) copy-start(bf16[2,4,48]{2,1,0:T(4,128)(2,1)} %param.20) | copy-start | bytes 2308
  160.3 153.2 %all-gather.27.cloned.1.call-start = ((), (), s32[]{:S(2)}) async-start(), calls=%async_computation.45 | async-start | bytes 2506752 | tf_op jit(solution)/shard_map/all_gather | solution.py:17
  162.1 155.1 %all-gather.29.cloned.1.call-start = ((), (), s32[]{:S(2)}) async-start(), calls=%async_computation.46 | async-start | bytes 2506752 | tf_op jit(solution)/shard_map/all_gather | solution.py:19
  163.8 211.2 %reduce-scatter.53.cloned.1.call-start = ((), (), s32[]{:S(2)}) async-start(), calls=%async_computation.33 | async-start | bytes 589824 | tf_op jit(solution)/shard_map/reduce_scatter | solution.py:30
  294.3 80.8 %copy-start.134 = (f32[768]{0:T(1024)}, f32[768]{0:T(1024)S(1)}, u32[]{:S(2)}) copy-start(f32[768]{0:T(1024)S(1)} %get-tuple-element.340) | copy-start | bytes 9220
  305.3 71.9 %copy-start.141 = (f32[768]{0:T(1024)}, f32[768]{0:T(1024)S(1)}, u32[]{:S(2)}) copy-start(f32[768]{0:T(1024)S(1)} %get-tuple-element.341) | copy-start | bytes 9220
  320.9 54.1 %reduce-scatter.45.cloned.1.call-start = ((), (), s32[]{:S(2)}) async-start(), calls=%async_computation.29 | async-start | bytes 589824 | tf_op jit(solution)/shard_map/reduce_scatter | solution.py:30
  329.7 71.8 %all-gather.31.cloned.1.call-start = ((), (), s32[]{:S(2)}) async-start(), calls=%async_computation.47 | async-start | bytes 1880064 | tf_op jit(solution)/shard_map/all_gather | solution.py:14
  330.5 202.4 %reduce-scatter.47.cloned.1.call-start = ((), (), s32[]{:S(2)}) async-start(), calls=%async_computation.30 | async-start | bytes 589824 | tf_op jit(solution)/shard_map/reduce_scatter | solution.py:30
  377.0 26.8 %copy-start.160 = (f32[128]{0:T(128)}, f32[128]{0:T(128)S(1)}, u32[]{:S(2)}) copy-start(f32[128]{0:T(128)S(1)} %broadcast_multiply_fusion.22) | copy-start | bytes 1540
  420.9 112.0 %reduce-scatter.55.cloned.1.call-start = ((), (), s32[]{:S(2)}) async-start(), calls=%async_computation.34 | async-start | bytes 589824 | tf_op jit(solution)/shard_map/reduce_scatter | solution.py:30
  430.5 107.9 %all-gather.33.cloned.1.call-start = ((), (), s32[]{:S(2)}) async-start(), calls=%async_computation.48 | async-start | bytes 2506752 | tf_op jit(solution)/shard_map/all_gather | solution.py:17
  431.2 141.5 %all-gather.35.cloned.1.call-start = ((), (), s32[]{:S(2)}) async-start(), calls=%async_computation.49 | async-start | bytes 2506752 | tf_op jit(solution)/shard_map/all_gather | solution.py:19
  431.8 154.7 %reduce-scatter.57.cloned.1.call-start = ((), (), s32[]{:S(2)}) async-start(), calls=%async_computation.35 | async-start | bytes 589824 | tf_op jit(solution)/shard_map/reduce_scatter | solution.py:30
  476.6 56.2 %copy-start.142 = (f32[768]{0:T(1024)S(1)}, f32[768]{0:T(1024)}, u32[]{:S(2)}) copy-start(f32[768]{0:T(1024)} %copy-done.141) | copy-start | bytes 9220
  576.5 18.0 reduce-scatter.49.cloned.1.call-start
  585.1 11.5 copy-start.143
  585.1 30.3 %reduce-scatter.67.cloned.1.call-start = ((), (), s32[]{:S(2)}) async-start(), calls=%async_computation.40 | async-start | bytes 589824 | tf_op jit(solution)/shard_map/reduce_scatter | solution.py:30
  605.3 20.1 reduce-scatter.59.cloned.1.call-start
  612.5 13.0 copy-start.165
  614.1 62.5 %reduce-scatter.69.cloned.1.call-start = ((), (), s32[]{:S(2)}) async-start(), calls=%async_computation.41 | async-start | bytes 589824 | tf_op jit(solution)/shard_map/reduce_scatter | solution.py:30
  663.4 22.2 reduce-scatter.61.cloned.1.call-start
  673.3 12.4 copy-start.161
  676.5 60.7 %reduce-scatter.63.cloned.1.call-start = ((), (), s32[]{:S(2)}) async-start(), calls=%async_computation.38 | async-start | bytes 589824 | tf_op jit(solution)/shard_map/reduce_scatter | solution.py:30
  696.9 40.4 %reduce-scatter.71.cloned.1.call-start = ((), (), s32[]{:S(2)}) async-start(), calls=%async_computation.42 | async-start | bytes 589824 | tf_op jit(solution)/shard_map/reduce_scatter | solution.py:30
  704.2 7.2 copy-start.152
  705.8 141.1 %reduce-scatter.89.cloned.1.call-start = ((), (), s32[]{:S(2)}) async-start(), calls=%async_computation.57 | async-start | bytes 835584
  713.9 259.9 %reduce-scatter.93.cloned.1.call-start = ((), (), s32[]{:S(2)}) async-start(), calls=%async_computation.59 | async-start | bytes 417792
  721.7 15.8 copy-start.135
  723.3 378.3 %reduce-scatter.87.cloned.1.call-start = ((), (), s32[]{:S(2)}) async-start(), calls=%async_computation.56 | async-start | bytes 835584
  727.8 500.7 %reduce-scatter.97.cloned.1.call-start = ((), (), s32[]{:S(2)}) async-start(), calls=%async_computation.61 | async-start | bytes 417792
  737.2 618.2 %reduce-scatter.91.cloned.1.call-start = ((), (), s32[]{:S(2)}) async-start(), calls=%async_computation.58 | async-start | bytes 417792
  757.1 725.3 %reduce-scatter.95.cloned.1.call-start = ((), (), s32[]{:S(2)}) async-start(), calls=%async_computation.60 | async-start | bytes 417792
  759.5 732.5 %reduce-scatter.73.cloned.1.call-start = ((), (), s32[]{:S(2)}) async-start(), calls=%async_computation.43 | async-start | bytes 589824 | tf_op jit(solution)/shard_map/reduce_scatter | solution.py:30
  763.3 739.9 %reduce-scatter.65.cloned.1.call-start = ((), (), s32[]{:S(2)}) async-start(), calls=%async_computation.39 | async-start | bytes 589824 | tf_op jit(solution)/shard_map/reduce_scatter | solution.py:30
  769.7 865.0 %reduce-scatter.77.cloned.1.call-start = ((), (), s32[]{:S(2)}) async-start(), calls=%async_computation.51 | async-start | bytes 1253376 | tf_op jit(solution)/shard_map/reduce_scatter | solution.py:334
  772.2 991.9 %reduce-scatter.75.cloned.1.call-start = ((), (), s32[]{:S(2)}) async-start(), calls=%async_computation.50 | async-start | bytes 1253376 | tf_op jit(solution)/shard_map/reduce_scatter | solution.py:334
  774.6 1273.5 %all-reduce.12.cloned.1.call-start = ((), (), s32[]{:S(2)}) async-start(), calls=%async_computation.62 | async-start | bytes 18874368
  796.5 1394.5 %reduce-scatter.81.cloned.1.call-start = ((), (), s32[]{:S(2)}) async-start(), calls=%async_computation.53 | async-start | bytes 5013504 | tf_op jit(solution)/shard_map/reduce_scatter | solution.py:335
  801.5 1532.9 %reduce-scatter.79.cloned.1.call-start = ((), (), s32[]{:S(2)}) async-start(), calls=%async_computation.52 | async-start | bytes 5013504 | tf_op jit(solution)/shard_map/reduce_scatter | solution.py:335
  806.7 1671.3 %reduce-scatter.85.cloned.1.call-start = ((), (), s32[]{:S(2)}) async-start(), calls=%async_computation.55 | async-start | bytes 5013504 | tf_op jit(solution)/shard_map/reduce_scatter | solution.py:337
  811.8 1809.4 %reduce-scatter.83.cloned.1.call-start = ((), (), s32[]{:S(2)}) async-start(), calls=%async_computation.54 | async-start | bytes 5013504 | tf_op jit(solution)/shard_map/reduce_scatter | solution.py:337
  817.0 30.8 %copy-start.46 = (bf16[256,1,384]{2,0,1:T(8,128)(2,1)S(1)}, bf16[256,1,384]{2,0,1:T(8,128)(2,1)}, u32[]{:S(2)}) copy-start(bf16[256,1,384]{2,0,1:T(8,128)(2,1)} %copy.291) | copy-start | bytes 589828
  817.0 30.7 %copy-start.47 = (bf16[256,1,384]{2,0,1:T(8,128)(2,1)S(1)}, bf16[256,1,384]{2,0,1:T(8,128)(2,1)}, u32[]{:S(2)}) copy-start(bf16[256,1,384]{2,0,1:T(8,128)(2,1)} %copy.289) | copy-start | bytes 589828
  817.0 30.7 %copy-start.48 = (bf16[256,1,384]{2,0,1:T(8,128)(2,1)S(1)}, bf16[256,1,384]{2,0,1:T(8,128)(2,1)}, u32[]{:S(2)}) copy-start(bf16[256,1,384]{2,0,1:T(8,128)(2,1)} %copy.290) | copy-start | bytes 589828
  817.0 30.8 %copy-start.68 = (bf16[256,1,384]{2,0,1:T(8,128)(2,1)S(1)}, bf16[256,1,384]{2,0,1:T(8,128)(2,1)}, u32[]{:S(2)}) copy-start(bf16[256,1,384]{2,0,1:T(8,128)(2,1)} %copy.305) | copy-start | bytes 589828
  817.0 30.8 %copy-start.70 = (bf16[256,1,384]{2,0,1:T(8,128)(2,1)S(1)}, bf16[256,1,384]{2,0,1:T(8,128)(2,1)}, u32[]{:S(2)}) copy-start(bf16[256,1,384]{2,0,1:T(8,128)(2,1)} %copy.303) | copy-start | bytes 589828
  817.1 30.8 %copy-start.72 = (bf16[256,1,384]{2,0,1:T(8,128)(2,1)S(1)}, bf16[256,1,384]{2,0,1:T(8,128)(2,1)}, u32[]{:S(2)}) copy-start(bf16[256,1,384]{2,0,1:T(8,128)(2,1)} %copy.304) | copy-start | bytes 589828
  817.1 412.2 %copy-start.75 = (bf16[256,1,384]{2,0,1:T(8,128)(2,1)S(1)}, bf16[256,1,384]{2,0,1:T(8,128)(2,1)}, u32[]{:S(2)}) copy-start(bf16[256,1,384]{2,0,1:T(8,128)(2,1)} %copy-done.73) | copy-start | bytes 589828
  817.1 412.2 %copy-start.78 = (bf16[256,1,384]{2,0,1:T(8,128)(2,1)S(1)}, bf16[256,1,384]{2,0,1:T(8,128)(2,1)}, u32[]{:S(2)}) copy-start(bf16[256,1,384]{2,0,1:T(8,128)(2,1)} %copy-done.76) | copy-start | bytes 589828
  817.1 412.2 %copy-start.81 = (bf16[256,1,384]{2,0,1:T(8,128)(2,1)S(1)}, bf16[256,1,384]{2,0,1:T(8,128)(2,1)}, u32[]{:S(2)}) copy-start(bf16[256,1,384]{2,0,1:T(8,128)(2,1)} %copy-done.79) | copy-start | bytes 589828
  818.6 410.9 %copy-start.50 = (bf16[256,1,384]{2,0,1:T(8,128)(2,1)S(1)}, bf16[256,1,384]{2,0,1:T(8,128)(2,1)}, u32[]{:S(2)}) copy-start(bf16[256,1,384]{2,0,1:T(8,128)(2,1)} %copy-done.49) | copy-start | bytes 589828
  818.6 410.9 %copy-start.52 = (bf16[256,1,384]{2,0,1:T(8,128)(2,1)S(1)}, bf16[256,1,384]{2,0,1:T(8,128)(2,1)}, u32[]{:S(2)}) copy-start(bf16[256,1,384]{2,0,1:T(8,128)(2,1)} %copy-done.51) | copy-start | bytes 589828
  818.6 410.9 %copy-start.54 = (bf16[256,1,384]{2,0,1:T(8,128)(2,1)S(1)}, bf16[256,1,384]{2,0,1:T(8,128)(2,1)}, u32[]{:S(2)}) copy-start(bf16[256,1,384]{2,0,1:T(8,128)(2,1)} %copy-done.53) | copy-start | bytes 589828
  819.5 672.5 %copy-start.34 = (f32[128,768]{1,0:T(8,128)S(1)}, f32[128,768]{1,0:T(8,128)}, u32[]{:S(2)}) copy-start(f32[128,768]{1,0:T(8,128)} %copy-done.33) | copy-start | bytes 1179652
  847.9 655.3 %copy-start.32 = (f32[128,768]{1,0:T(8,128)S(1)}, f32[128,768]{1,0:T(8,128)}, u32[]{:S(2)}) copy-start(f32[128,768]{1,0:T(8,128)} %get-tuple-element.362) | copy-start | bytes 1179652
  (167 other events, 395.2 us)
Sparse Core Ops, SparseCore 0:
  11.3 62.2 all-gather.24
  153.9 3.6 reduce-scatter.42
  160.4 9.0 reduce-scatter.50
  172.8 66.4 all-gather.26
  242.5 61.0 all-gather.28
  321.1 5.6 reduce-scatter.52
  329.8 8.6 reduce-scatter.44
  341.2 60.2 all-gather.30
  421.0 6.5 reduce-scatter.46
  430.6 8.5 reduce-scatter.54
  442.6 65.2 all-gather.32
  510.5 62.1 all-gather.34
  576.6 6.1 reduce-scatter.56
  585.5 8.9 reduce-scatter.48
  605.5 8.9 reduce-scatter.66
  616.5 8.9 reduce-scatter.58
  663.5 8.9 reduce-scatter.68
  676.7 8.9 reduce-scatter.60
  697.1 8.9 reduce-scatter.62
  708.1 8.9 reduce-scatter.70
  721.8 125.0 reduce-scatter.88
  851.5 122.2 reduce-scatter.92
  978.6 123.0 reduce-scatter.86
  1106.1 122.3 reduce-scatter.96
  1233.1 122.2 reduce-scatter.90
  1360.0 122.3 reduce-scatter.94
  1485.0 6.9 reduce-scatter.72
  1494.2 8.9 reduce-scatter.64
  1507.9 126.7 reduce-scatter.76
  1639.3 124.6 reduce-scatter.74
  1770.4 277.6 all-reduce.11
  2053.3 137.6 reduce-scatter.80
  2196.0 138.3 reduce-scatter.78
  2339.6 138.2 reduce-scatter.84
  2483.1 138.0 reduce-scatter.82
where the time goes:
time: 2640 us; the launch traced here: 2630 us
  waiting for transfers between devices  1820 us (69%)
  blocking collectives  446 us (17%)
  local copies, waits for them, and re-layouts  141 us (5%)
  matrix products  128 us (5%)
  other arithmetic  79.9 us (3%)
    unnamed x42, waiting for transfers between devices  901 us
    reduce_scatter x2, waiting for transfers between devices, on_device(): lax.psum_scatter(layer_grads[5], 'dp', scatter_dimension=1, tiled=True)  285 us
    reduce_scatter x2, waiting for transfers between devices, on_device(): lax.psum_scatter(layer_grads[3], 'dp', scatter_dimension=0, tiled=True)  283 us
    reduce_scatter x2, waiting for transfers between devices, on_device(): lax.psum_scatter(layer_grads[2], 'dp', scatter_dimension=1, tiled=True)  259 us
    all_gather x2, blocking collectives, fetch_each(): lax.all_gather(layer_weights[2], 'dp', axis=1, tiled=True)  85.4 us
    all_gather x2, blocking collectives, fetch_each(): lax.all_gather(layer_weights[7], 'dp', axis=1, tiled=True)  83.4 us
    all_gather x2, blocking collectives, fetch_each(): lax.all_gather(layer_weights[1], 'dp', axis=2, tiled=True)  81 us
    all_gather x2, blocking collectives, fetch_each(): lax.all_gather(layer_weights[6], 'dp', axis=1, tiled=True)  79.1 us
  transfers between devices with their start and end apart: 35, of which 20 were waited for; matrix products, arithmetic and copies ran while one was open for 9% of the time, Pallas kernels for 0%

commit v1 on v0

--- a/solution.py
+++ b/solution.py
@@ -9,11 +9,44 @@
 DENSITY_SCALE = 0.3989422804014327
 
 
+def _run_pairs_all(z, dim_i):
+    z_new = list(z.shape[1:])
+    z_new[dim_i] *= z.shape[0]
+    frame_out = jnp.moveaxis(z, 0, dim_i).reshape(z_new)
+    return frame_out
+
+
+def wrap_windows(u, mesh_name, on_dim):
+    how_many = jax.lax.psum(1, axis_name=mesh_name)
+    runs = []
+    for tick in range(how_many):
+        runs.append((tick, (tick + 1) % how_many))
+    sheets = []
+    for d, it in runs:
+        sheets.append((it, d))
+    e_next, small = ([], [])
+    for rr in range(how_many - 1):
+        if rr % 2 == 0:
+            x_now = jax.lax.ppermute(e_next[-1] if e_next else u, axis_name=mesh_name, perm=runs)
+            e_next.append(x_now)
+        else:
+            small.append(
+                jax.lax.ppermute(small[-1] if small else u, axis_name=mesh_name, perm=sheets)
+            )
+    all_rows = jnp.stack([*e_next[::-1], u, *small], 0)
+    later = jax.lax.axis_index(mesh_name)
+    taken_in = len(e_next)
+    mid_arr = later - taken_in
+    all_rows = all_rows[(jnp.arange(how_many) - mid_arr) % how_many]
+    side_arr = _run_pairs_all(all_rows, on_dim)
+    return side_arr
+
+
 def fetch_each(layer_weights):
     return (
         lax.all_gather(layer_weights[0], "dp", axis=1, tiled=True),
         lax.all_gather(layer_weights[1], "dp", axis=2, tiled=True),
-        lax.all_gather(layer_weights[2], "dp", axis=1, tiled=True),
+        wrap_windows(layer_weights[2], "dp", 1),
         lax.all_gather(layer_weights[3], "dp", axis=0, tiled=True),
         lax.all_gather(layer_weights[4], "dp", axis=1, tiled=True),
         lax.all_gather(layer_weights[5], "dp", axis=1, tiled=True),

time: 2640 us -> 2680 us (1.015)
  blocking collectives: 446 us -> 364 us
  starting transfers between devices: 1.62 us -> 78.5 us
  waiting for transfers between devices: 1820 us -> 1850 us
    all_gather x2 -> x0, blocking collectives: 85.4 us -> none  [fetch_each(): lax.all_gather(layer_weights[2], 'dp', axis=1, tiled=True)]
    ppermute x0 -> x30, starting transfers between devices: none -> 76.8 us  [the longest x14 76.6 us: wrap_windows(): jax.lax.ppermute(small[-1] if small else u, axis_name=mesh_name, perm=she...]
  transfers between devices with their start and end apart: 35 -> 65, of which waited for: 20 -> 39; matrix products, arithmetic and copies ran while one was open for 9% -> 9% of each run, Pallas kernels for 0% -> 0%
where the time goes in v1:
time: 2680 us; the launch traced here: 2670 us
  waiting for transfers between devices  1850 us (69%)
  blocking collectives  364 us (14%)
  local copies, waits for them, and re-layouts  149 us (6%)
  matrix products  123 us (5%)
  other arithmetic  79.3 us (3%)
  starting transfers between devices  78.5 us (3%)
    unnamed x42, waiting for transfers between devices  907 us
    reduce_scatter x2, waiting for transfers between devices, on_device(): lax.psum_scatter(layer_grads[5], 'dp', scatter_dimension=1, tiled=True)  285 us
    reduce_scatter x2, waiting for transfers between devices, on_device(): lax.psum_scatter(layer_grads[3], 'dp', scatter_dimension=0, tiled=True)  283 us
    reduce_scatter x2, waiting for transfers between devices, on_device(): lax.psum_scatter(layer_grads[2], 'dp', scatter_dimension=1, tiled=True)  259 us
    all_gather x2, blocking collectives, fetch_each(): lax.all_gather(layer_weights[1], 'dp', axis=2, tiled=True)  84.8 us
    all_gather x2, blocking collectives, fetch_each(): lax.all_gather(layer_weights[7], 'dp', axis=1, tiled=True)  82.3 us
    all_gather x2, blocking collectives, fetch_each(): lax.all_gather(layer_weights[6], 'dp', axis=1, tiled=True)  80.7 us
    unnamed x2, blocking collectives  78.3 us
  transfers between devices with their start and end apart: 65, of which 39 were waited for; matrix products, arithmetic and copies ran while one was open for 9% of the time, Pallas kernels for 0%

profile of v1, /device:TPU:0, one launch (start us, length us, event | category | flops | bytes accessed | tf_op | source)
XLA Modules:
  0.0 2666.8 jit_solution(2041251774721417736)
XLA Ops:
  8.0 7.0 collective-permute-start.8
  20.0 42.5 %all-gather.2 = bf16[1,2,1,384]{2,1,0,3:T(2,128)(2,1)S(1)} all-gather(bf16[1,2,1,24]{2,1,0,3:T(2,128)(2,1)S(1)} %copy.360), channel_id=4, replica_groups=mesh['dp'=16,'tensor'=2] {'dp'}, dimensions={3}, use_global_device_ids=true | all-gather | bytes 1632 | tf_op jit(solution)/shard_map/all_gather | solution.py:48
  64.4 42.3 %all-gather.9 = bf16[1,2,1,384]{2,1,0,3:T(2,128)(2,1)S(1)} all-gather(bf16[1,2,1,24]{2,1,0,3:T(2,128)(2,1)S(1)} %copy.363), channel_id=11, replica_groups=mesh['dp'=16,'tensor'=2] {'dp'}, dimensions={3}, use_global_device_ids=true | all-gather | bytes 1632 | tf_op jit(solution)/shard_map/all_gather | solution.py:48
  108.7 5.6 collective-permute-start.9
  116.0 5.9 collective-permute-start.10
  123.5 5.9 collective-permute-start.11
  131.1 6.0 collective-permute-start.12
  139.7 5.6 collective-permute-start.13
  147.5 5.6 collective-permute-start.14
  153.4 7.3 collective-permute-done.22
  180.6 37.9 %all-reduce.9 = (bf16[1536]{0:T(1024)(128)(2,1)S(1)}, bf16[1536]{0:T(1024)(128)(2,1)}) all-reduce(bf16[1536]{0:T(1024)(128)(2,1)S(1)} %dynamic-update-slice, bf16[1536]{0:T(1024)(128)(2,1)S(1)} %dynamic-update-slice.1), channel_id=8, replica_groups=mesh['dp'=16,'tensor'=2] {'dp'}, use_global_device_ids=true, to_apply=%add | all-reduce | flops 3072 | bytes 12288
  221.0 40.5 %all-gather.3 = bf16[1,4,768]{1,0,2:T(2,128)(2,1)S(1)} all-gather(bf16[1,4,48]{1,0,2:T(2,128)(2,1)S(1)} %copy.361), channel_id=5, replica_groups=mesh['dp'=16,'tensor'=2] {'dp'}, dimensions={2}, use_global_device_ids=true | all-gather | bytes 6528 | tf_op jit(solution)/shard_map/all_gather | solution.py:54
  261.9 40.7 %all-gather.4 = bf16[1,2,768]{1,0,2:T(2,128)(2,1)S(1)} all-gather(bf16[1,2,48]{1,0,2:T(2,128)(2,1)} %copy.362), channel_id=6, replica_groups=mesh['dp'=16,'tensor'=2] {'dp'}, dimensions={2}, use_global_device_ids=true | all-gather | bytes 3264 | tf_op jit(solution)/shard_map/all_gather | solution.py:53
  302.6 4.6 fusion.176
  307.2 11.0 slice_reduce_fusion.4
  326.4 3.6 convolution_add_fusion.5
  330.1 3.8 fusion.121
  336.2 3.8 multiply_convert_fusion.7
  343.3 3.5 collective-permute-done.23
  347.4 4.3 collective-permute-start.24
  354.0 5.9 collective-permute-start.25
  362.1 5.9 collective-permute-start.26
  370.3 5.9 collective-permute-start.27
  377.9 6.0 collective-permute-start.28
  386.0 6.1 collective-permute-start.29
  410.7 28.1 %all-gather.29.cloned.1.call-done = bf16[1,3,768,384]{3,2,1,0:T(8,128)(2,1)} async-done(((bf16[1,3,48,384]{3,2,1,0:T(8,128)(2,1)}), bf16[1,3,768,384]{3,2,1,0:T(8,128)(2,1)}) %all-gather.29.cloned.1.call-update) | async-done | bytes 1769488 | tf_op jit(solution)/shard_map/all_gather | solution.py:47
  471.7 41.8 %all-gather.10 = bf16[1,4,768]{1,0,2:T(2,128)(2,1)S(1)} all-gather(bf16[1,4,48]{1,0,2:T(2,128)(2,1)} %copy.364), channel_id=12, replica_groups=mesh['dp'=16,'tensor'=2] {'dp'}, dimensions={2}, use_global_device_ids=true | all-gather | bytes 6528 | tf_op jit(solution)/shard_map/all_gather | solution.py:54
  513.9 40.0 %all-gather.11 = bf16[1,2,768]{1,0,2:T(2,128)(2,1)S(1)} all-gather(bf16[1,2,48]{1,0,2:T(2,128)(2,1)} %copy.365), channel_id=13, replica_groups=mesh['dp'=16,'tensor'=2] {'dp'}, dimensions={2}, use_global_device_ids=true | all-gather | bytes 3264 | tf_op jit(solution)/shard_map/all_gather | solution.py:53
  553.9 4.6 fusion.174
  558.5 11.8 slice_reduce_fusion
  575.8 3.7 convolution_add_fusion.4
  579.6 30.3 %all-gather.33.cloned.1.call-done = bf16[1,1536,768]{1,2,0:T(8,128)(2,1)} async-done(((bf16[1,1536,48]{1,2,0:T(8,128)(2,1)}), bf16[1,1536,768]{1,2,0:T(8,128)(2,1)}) %all-gather.33.cloned.1.call-update) | async-done | bytes 2359312 | tf_op jit(solution)/shard_map/all_gather | solution.py:52
  609.8 3.8 fusion.133
  616.0 3.9 multiply_convert_fusion.6
  623.7 7.9 reduce-scatter.49.cloned.1.call-done
  644.9 3.9 convert_reduce_fusion.1
  655.8 6.8 reduce-scatter.59.cloned.1.call-done
  662.6 3.4 fusion.213
  697.3 3.2 fusion.100
  710.5 3.3 fusion.103
  716.9 5.9 reduce-scatter.61.cloned.1.call-done
  736.5 3.9 convert_reduce_fusion.2
  806.3 3.0 fusion.109
  816.3 4.0 copy.318
  823.1 3.9 copy.315
  839.3 3.0 convolution_add_fusion
  844.4 3.1 convolution_add_fusion.1
  850.1 34.1 %reduce-scatter.89.cloned.1.call-done = f32[96,1]{1,0:T(8,128)} async-done(((f32[1536,1]{1,0:T(8,128)}), f32[96,1]{1,0:T(8,128)}) %reduce-scatter.89.cloned.1.call-update) | async-done | bytes 400
  885.4 125.7 %reduce-scatter.93.cloned.1.call-done = f32[48,2]{1,0:T(8,128)} async-done(((f32[768,2]{1,0:T(8,128)}), f32[48,2]{1,0:T(8,128)}) %reduce-scatter.93.cloned.1.call-update) | async-done | bytes 400
  1011.9 127.0 %reduce-scatter.87.cloned.1.call-done = f32[96,1]{1,0:T(8,128)} async-done(((f32[1536,1]{1,0:T(8,128)}), f32[96,1]{1,0:T(8,128)}) %reduce-scatter.87.cloned.1.call-update) | async-done | bytes 400
  1140.3 125.3 %reduce-scatter.97.cloned.1.call-done = f32[48,4]{1,0:T(8,128)} async-done(((f32[768,4]{1,0:T(8,128)}), f32[48,4]{1,0:T(8,128)}) %reduce-scatter.97.cloned.1.call-update) | async-done | bytes 784
  1266.7 40.4 %all-reduce.6 = (f32[2,1,384]{2,0,1:T(2,128)S(1)}, f32[2,1,384]{2,0,1:T(2,128)S(1)}) all-reduce(f32[2,1,384]{2,0,1:T(2,128)S(1)} %fusion.199, f32[2,1,384]{2,0,1:T(2,128)S(1)} %fusion.198), channel_id=53, replica_groups=mesh['dp'=16,'tensor'=2] {'dp'}, use_global_device_ids=true, to_apply=%region_73.74.clone | all-reduce | flops 1536 | bytes 12288
  1307.9 84.7 %reduce-scatter.91.cloned.1.call-done = f32[48,2]{1,0:T(8,128)} async-done(((f32[768,2]{1,0:T(8,128)}), f32[48,2]{1,0:T(8,128)}) %reduce-scatter.91.cloned.1.call-update) | async-done | bytes 400
  1393.4 126.0 %reduce-scatter.95.cloned.1.call-done = f32[48,4]{1,0:T(8,128)} async-done(((f32[768,4]{1,0:T(8,128)}), f32[48,4]{1,0:T(8,128)}) %reduce-scatter.95.cloned.1.call-update) | async-done | bytes 784
  1520.2 3.1 all-reduce.8
  1523.2 5.7 reduce-scatter.73.cloned.1.call-done
  1529.9 10.2 reduce-scatter.65.cloned.1.call-done
  1542.0 129.7 %reduce-scatter.77.cloned.1.call-done = f32[384,48]{0,1:T(8,128)} async-done(((f32[384,768]{0,1:T(8,128)}), f32[384,48]{0,1:T(8,128)}) %reduce-scatter.77.cloned.1.call-update) | async-done | bytes 73744 | tf_op jit(solution)/shard_map/reduce_scatter | solution.py:367
  1671.7 129.3 %reduce-scatter.75.cloned.1.call-done = f32[384,48]{0,1:T(8,128)} async-done(((f32[384,768]{0,1:T(8,128)}), f32[384,48]{0,1:T(8,128)}) %reduce-scatter.75.cloned.1.call-update) | async-done | bytes 73744 | tf_op jit(solution)/shard_map/reduce_scatter | solution.py:367
  1802.6 282.4 %all-reduce.12.cloned.1.call-done = (f32[3,768,384]{2,0,1:T(4,128)}, f32[3,768,384]{2,0,1:T(4,128)}) async-done(((f32[3,768,384]{2,0,1:T(4,128)}, f32[3,768,384]{2,0,1:T(4,128)}), (f32[3,768,384]{2,0,1:T(4,128)}, f32[3,768,384]{2,0,1:T(4,128)})) %all-reduce.12.cloned.1.call-update) | async-done | bytes 7077904
  2087.9 140.0 %reduce-scatter.81.cloned.1.call-done = f32[48,1536]{1,0:T(8,128)} async-done(((f32[768,1536]{1,0:T(8,128)}), f32[48,1536]{1,0:T(8,128)}) %reduce-scatter.81.cloned.1.call-update) | async-done | bytes 294928 | tf_op jit(solution)/shard_map/reduce_scatter | solution.py:368
  2227.9 143.5 %reduce-scatter.79.cloned.1.call-done = f32[48,1536]{1,0:T(8,128)} async-done(((f32[768,1536]{1,0:T(8,128)}), f32[48,1536]{1,0:T(8,128)}) %reduce-scatter.79.cloned.1.call-update) | async-done | bytes 294928 | tf_op jit(solution)/shard_map/reduce_scatter | solution.py:368
  2373.3 141.5 %reduce-scatter.85.cloned.1.call-done = f32[1536,48]{0,1:T(8,128)} async-done(((f32[1536,768]{0,1:T(8,128)}), f32[1536,48]{0,1:T(8,128)}) %reduce-scatter.85.cloned.1.call-update) | async-done | bytes 294928 | tf_op jit(solution)/shard_map/reduce_scatter | solution.py:370
  2514.8 143.1 %reduce-scatter.83.cloned.1.call-done = f32[1536,48]{0,1:T(8,128)} async-done(((f32[1536,768]{0,1:T(8,128)}), f32[1536,48]{0,1:T(8,128)}) %reduce-scatter.83.cloned.1.call-update) | async-done | bytes 294928 | tf_op jit(solution)/shard_map/reduce_scatter | solution.py:370
  (874 shorter events, 315.1 us)
Async XLA Ops:
  7.2 155.2 %all-gather.23.cloned.1.call-start = ((), (), s32[]{:S(2)}) async-start(), calls=%async_computation.44 | async-start | bytes 1880064 | tf_op jit(solution)/shard_map/all_gather | solution.py:47
  8.0 100.7 %collective-permute-start.8 = (bf16[384,48]{0,1:T(8,128)(2,1)S(1)}, bf16[384,48]{0,1:T(8,128)(2,1)S(1)}, u32[]{:S(2)}, u32[]{:S(2)}) collective-permute-start(bf16[384,48]{0,1:T(8,128)(2,1)S(1)} %get-tuple-element.419), channel_id=1, source_target_pairs={{2,0},{4,2},{6,4},{8,6},{10,8},{12,10},{14,12},{16,14},{18,16},{20... | collective-permute-start | bytes 110600 | tf_op jit(solution)/shard_map/ppermute | solution.py:34
  15.0 47.6 %collective-permute-start = (bf16[384,48]{0,1:T(8,128)(2,1)S(1)}, bf16[384,48]{0,1:T(8,128)(2,1)S(1)}, u32[]{:S(2)}, u32[]{:S(2)}) collective-permute-start(bf16[384,48]{0,1:T(8,128)(2,1)S(1)} %get-tuple-element.419), channel_id=1, source_target_pairs={{0,2},{2,4},{4,6},{6,8},{8,10},{10,12},{12,14},{14,16},{16,18},{18... | collective-permute-start | bytes 110600 | tf_op jit(solution)/shard_map/ppermute | solution.py:30
  15.1 91.9 %collective-permute-start.15 = (bf16[384,48]{0,1:T(8,128)(2,1)S(1)}, bf16[384,48]{0,1:T(8,128)(2,1)S(1)}, u32[]{:S(2)}, u32[]{:S(2)}) collective-permute-start(bf16[384,48]{0,1:T(8,128)(2,1)S(1)} %get-tuple-element.418), channel_id=1, source_target_pairs={{0,2},{2,4},{4,6},{6,8},{8,10},{10,12},{12,14},{14,16},{16,18},{18... | collective-permute-start | bytes 110600 | tf_op jit(solution)/shard_map/ppermute | solution.py:30
  16.7 301.5 %reduce-scatter.43.cloned.1.call-start = ((), (), s32[]{:S(2)}) async-start(), calls=%async_computation.28 | async-start | bytes 589824 | tf_op jit(solution)/shard_map/reduce_scatter | solution.py:63
  62.7 44.3 %collective-permute-start.1 = (bf16[384,48]{0,1:T(8,128)(2,1)S(1)}, bf16[384,48]{0,1:T(8,128)(2,1)S(1)}, u32[]{:S(2)}, u32[]{:S(2)}) collective-permute-start(bf16[384,48]{0,1:T(8,128)(2,1)S(1)} %collective-permute-done), channel_id=1, source_target_pairs={{0,2},{2,4},{4,6},{6,8},{8,10},{10,12},{12,14},{14,16},{16,18},{18... | collective-permute-start | bytes 110600 | tf_op jit(solution)/shard_map/ppermute | solution.py:30
  106.9 7.6 collective-permute-start.16
  107.0 8.0 collective-permute-start.2
  108.7 7.2 collective-permute-start.9
  114.5 7.6 collective-permute-start.17
  115.0 7.6 collective-permute-start.3
  116.0 7.6 collective-permute-start.10
  122.1 7.6 collective-permute-start.18
  122.5 7.6 collective-permute-start.4
  123.5 7.6 collective-permute-start.11
  129.6 7.6 collective-permute-start.19
  130.1 7.6 collective-permute-start.5
  131.1 8.6 collective-permute-start.12
  137.2 8.1 collective-permute-start.20
  137.6 7.7 collective-permute-start.6
  139.7 7.8 collective-permute-start.13
  145.3 7.8 collective-permute-start.21
  145.3 7.9 collective-permute-start.7
  147.5 13.4 collective-permute-start.14
  153.1 7.6 collective-permute-start.22
  171.1 148.8 %reduce-scatter.51.cloned.1.call-start = ((), (), s32[]{:S(2)}) async-start(), calls=%async_computation.32 | async-start | bytes 589824 | tf_op jit(solution)/shard_map/reduce_scatter | solution.py:63
  176.2 150.2 %all-gather.25.cloned.1.call-start = ((), (), s32[]{:S(2)}) async-start(), calls=%async_computation.45 | async-start | bytes 2506752 | tf_op jit(solution)/shard_map/all_gather | solution.py:50
  177.0 153.0 %all-gather.27.cloned.1.call-start = ((), (), s32[]{:S(2)}) async-start(), calls=%async_computation.46 | async-start | bytes 2506752 | tf_op jit(solution)/shard_map/all_gather | solution.py:52
  178.8 224.8 %reduce-scatter.53.cloned.1.call-start = ((), (), s32[]{:S(2)}) async-start(), calls=%async_computation.33 | async-start | bytes 589824 | tf_op jit(solution)/shard_map/reduce_scatter | solution.py:63
  333.8 69.8 %reduce-scatter.45.cloned.1.call-start = ((), (), s32[]{:S(2)}) async-start(), calls=%async_computation.29 | async-start | bytes 589824 | tf_op jit(solution)/shard_map/reduce_scatter | solution.py:63
  342.6 96.2 %all-gather.29.cloned.1.call-start = ((), (), s32[]{:S(2)}) async-start(), calls=%async_computation.47 | async-start | bytes 1880064 | tf_op jit(solution)/shard_map/all_gather | solution.py:47
  347.4 5.9 collective-permute-start.24
  354.0 7.6 collective-permute-start.25
  362.1 7.6 collective-permute-start.26
  370.3 7.6 collective-permute-start.27
  377.9 8.1 collective-permute-start.28
  383.9 186.4 %reduce-scatter.47.cloned.1.call-start = ((), (), s32[]{:S(2)}) async-start(), calls=%async_computation.30 | async-start | bytes 589824 | tf_op jit(solution)/shard_map/reduce_scatter | solution.py:63
  386.0 14.4 collective-permute-start.29
  458.1 112.3 %reduce-scatter.55.cloned.1.call-start = ((), (), s32[]{:S(2)}) async-start(), calls=%async_computation.34 | async-start | bytes 589824 | tf_op jit(solution)/shard_map/reduce_scatter | solution.py:63
  467.7 108.2 %all-gather.31.cloned.1.call-start = ((), (), s32[]{:S(2)}) async-start(), calls=%async_computation.48 | async-start | bytes 2506752 | tf_op jit(solution)/shard_map/all_gather | solution.py:50
  468.4 141.4 %all-gather.33.cloned.1.call-start = ((), (), s32[]{:S(2)}) async-start(), calls=%async_computation.49 | async-start | bytes 2506752 | tf_op jit(solution)/shard_map/all_gather | solution.py:52
  469.0 154.7 %reduce-scatter.57.cloned.1.call-start = ((), (), s32[]{:S(2)}) async-start(), calls=%async_computation.35 | async-start | bytes 589824 | tf_op jit(solution)/shard_map/reduce_scatter | solution.py:63
  613.6 18.0 reduce-scatter.49.cloned.1.call-start
  622.3 30.3 %reduce-scatter.67.cloned.1.call-start = ((), (), s32[]{:S(2)}) async-start(), calls=%async_computation.40 | async-start | bytes 589824 | tf_op jit(solution)/shard_map/reduce_scatter | solution.py:63
  642.5 20.1 reduce-scatter.59.cloned.1.call-start
  651.3 62.6 %reduce-scatter.69.cloned.1.call-start = ((), (), s32[]{:S(2)}) async-start(), calls=%async_computation.41 | async-start | bytes 589824 | tf_op jit(solution)/shard_map/reduce_scatter | solution.py:63
  700.6 22.2 reduce-scatter.61.cloned.1.call-start
  713.8 60.7 %reduce-scatter.63.cloned.1.call-start = ((), (), s32[]{:S(2)}) async-start(), calls=%async_computation.38 | async-start | bytes 589824 | tf_op jit(solution)/shard_map/reduce_scatter | solution.py:63
  734.1 40.4 %reduce-scatter.71.cloned.1.call-start = ((), (), s32[]{:S(2)}) async-start(), calls=%async_computation.42 | async-start | bytes 589824 | tf_op jit(solution)/shard_map/reduce_scatter | solution.py:63
  742.9 141.3 %reduce-scatter.89.cloned.1.call-start = ((), (), s32[]{:S(2)}) async-start(), calls=%async_computation.57 | async-start | bytes 835584
  751.0 260.0 %reduce-scatter.93.cloned.1.call-start = ((), (), s32[]{:S(2)}) async-start(), calls=%async_computation.59 | async-start | bytes 417792
  760.5 378.4 %reduce-scatter.87.cloned.1.call-start = ((), (), s32[]{:S(2)}) async-start(), calls=%async_computation.56 | async-start | bytes 835584
  765.0 500.6 %reduce-scatter.97.cloned.1.call-start = ((), (), s32[]{:S(2)}) async-start(), calls=%async_computation.61 | async-start | bytes 417792
  774.4 618.1 %reduce-scatter.91.cloned.1.call-start = ((), (), s32[]{:S(2)}) async-start(), calls=%async_computation.58 | async-start | bytes 417792
  794.0 725.4 %reduce-scatter.95.cloned.1.call-start = ((), (), s32[]{:S(2)}) async-start(), calls=%async_computation.60 | async-start | bytes 417792
  798.0 731.0 %reduce-scatter.73.cloned.1.call-start = ((), (), s32[]{:S(2)}) async-start(), calls=%async_computation.43 | async-start | bytes 589824 | tf_op jit(solution)/shard_map/reduce_scatter | solution.py:63
  802.3 737.8 %reduce-scatter.65.cloned.1.call-start = ((), (), s32[]{:S(2)}) async-start(), calls=%async_computation.39 | async-start | bytes 589824 | tf_op jit(solution)/shard_map/reduce_scatter | solution.py:63
  809.3 862.4 %reduce-scatter.77.cloned.1.call-start = ((), (), s32[]{:S(2)}) async-start(), calls=%async_computation.51 | async-start | bytes 1253376 | tf_op jit(solution)/shard_map/reduce_scatter | solution.py:367
  811.8 989.2 %reduce-scatter.75.cloned.1.call-start = ((), (), s32[]{:S(2)}) async-start(), calls=%async_computation.50 | async-start | bytes 1253376 | tf_op jit(solution)/shard_map/reduce_scatter | solution.py:367
  814.2 1270.8 %all-reduce.12.cloned.1.call-start = ((), (), s32[]{:S(2)}) async-start(), calls=%async_computation.62 | async-start | bytes 18874368
  827.1 1400.8 %reduce-scatter.81.cloned.1.call-start = ((), (), s32[]{:S(2)}) async-start(), calls=%async_computation.53 | async-start | bytes 5013504 | tf_op jit(solution)/shard_map/reduce_scatter | solution.py:368
  832.2 1539.2 %reduce-scatter.79.cloned.1.call-start = ((), (), s32[]{:S(2)}) async-start(), calls=%async_computation.52 | async-start | bytes 5013504 | tf_op jit(solution)/shard_map/reduce_scatter | solution.py:368
  837.3 1677.5 %reduce-scatter.85.cloned.1.call-start = ((), (), s32[]{:S(2)}) async-start(), calls=%async_computation.55 | async-start | bytes 5013504 | tf_op jit(solution)/shard_map/reduce_scatter | solution.py:370
  842.4 1815.5 %reduce-scatter.83.cloned.1.call-start = ((), (), s32[]{:S(2)}) async-start(), calls=%async_computation.54 | async-start | bytes 5013504 | tf_op jit(solution)/shard_map/reduce_scatter | solution.py:370
  (211 other events, 5350.8 us)
Sparse Core Ops, SparseCore 0:
  16.8 61.7 all-gather.22
  171.2 3.6 reduce-scatter.42
  177.7 8.9 reduce-scatter.50
  189.9 66.1 all-gather.24
  258.7 61.7 all-gather.26
  334.0 4.2 reduce-scatter.52
  342.7 7.3 reduce-scatter.44
  384.1 54.6 all-gather.28
  458.2 6.5 reduce-scatter.46
  467.8 8.5 reduce-scatter.54
  479.8 65.1 all-gather.30
  547.6 62.1 all-gather.32
  613.7 6.1 reduce-scatter.56
  622.6 8.9 reduce-scatter.48
  642.6 8.9 reduce-scatter.66
  653.7 8.9 reduce-scatter.58
  700.7 8.9 reduce-scatter.68
  713.9 8.8 reduce-scatter.60
  734.3 8.9 reduce-scatter.62
  745.3 8.9 reduce-scatter.70
  759.0 125.1 reduce-scatter.88
  888.8 122.1 reduce-scatter.92
  1015.8 123.0 reduce-scatter.86
  1143.4 122.1 reduce-scatter.96
  1270.3 122.2 reduce-scatter.90
  1397.1 122.2 reduce-scatter.94
  1522.0 6.8 reduce-scatter.72
  1531.2 8.9 reduce-scatter.64
  1544.9 126.7 reduce-scatter.76
  1676.3 124.6 reduce-scatter.74
  1807.4 277.5 all-reduce.11
  2090.2 137.6 reduce-scatter.80
  2232.9 138.4 reduce-scatter.78
  2376.6 138.1 reduce-scatter.84
  2519.9 137.9 reduce-scatter.82
